TPU v7x, 32 devices: a whole 2x2x4 slice. The times are simulated.
32 devices in a mesh: seq: 2 (over x), ctx: 16 (over z, y, core).
Axes of the slice: x: 2, y: 2, z: 4, core: 2. Of those that a mesh axis runs over, the one named last changes fastest.
Arguments:
- inputs: bfloat16 [2, 2048, 768], P('seq', 'ctx'), may hold values from -6 to 6
- lengths: int32 [2], P('seq'), may hold values from 512 to 2048, as said below
- cotangent: bfloat16 [2, 2048, 768], P('seq', 'ctx'), may hold values from -6 to 6
- w_qkv: bfloat16 [768, 2304], P(('seq', 'ctx')), may hold values from -0.21875 to 0.21875
- w_out: bfloat16 [768, 768], P(('seq', 'ctx')), may hold values from -6 to 6
- w_in: bfloat16 [768, 3072], P(('seq', 'ctx')), may hold values from -0.21875 to 0.21875
- w_back: bfloat16 [3072, 768], P(('seq', 'ctx')), may hold values from -0.109375 to 0.109375
- vectors: bfloat16 [768, 8], P(('seq', 'ctx')), may hold values from -1 to 2
- ffn_bias: bfloat16 [3072], P(('seq', 'ctx')), may hold values from -2 to 2
Outputs:
- result: bfloat16 [2, 2048, 768], P('seq', 'ctx')
- grad_inputs: float32 [2, 2048, 768], P('seq', 'ctx')
- grad_w_qkv: float32 [768, 2304], P(('seq', 'ctx'))
- grad_w_out: float32 [768, 768], P(('seq', 'ctx'))
- grad_w_in: float32 [768, 3072], P(('seq', 'ctx'))
- grad_w_back: float32 [3072, 768], P(('seq', 'ctx'))
- grad_vectors: float32 [768, 8], P(('seq', 'ctx'))
- grad_ffn_bias: float32 [3072], P(('seq', 'ctx'))
Inputs may be any that keep to these rules, and one draw needn't show every extreme that they name: `lengths`: one sequence of each draw is full.
All inputs are finite; a program needn't handle non-finite values.
Results may differ from a plain program's by a relative error of at most 0.025.
Values may be sent and summed in bfloat16 or wider, within the bound.
A program may use at most 448 MiB of HBM per device.

v0:
```python
import jax
import jax.numpy as jnp
from jax import lax
from jax.sharding import PartitionSpec as P

HEADS = 12
EPSILON = 1e-12
MASKED = -1e30


def layer_norm(values_in, norm_gain, norm_shift):
    average = jnp.mean(values_in, axis=-1, keepdims=True)
    centred = values_in - average
    spread = jnp.mean(centred * centred, axis=-1, keepdims=True)
    return centred * lax.rsqrt(spread + EPSILON) * norm_gain + norm_shift


def gelu_exact(values_in):
    return jax.nn.gelu(values_in, approximate=False)


def key_spans(extent_all):
    number_parts = min(8, max(1, -(-extent_all // 2048)))
    span_size = -(-extent_all // number_parts)
    return [
        (offset, min(span_size, extent_all - offset)) for offset in range(0, extent_all, span_size)
    ]


def to_heads(row_block, head_count):
    row_total = row_block.shape[0]
    return row_block.reshape(row_total, head_count, -1).transpose(1, 0, 2)


def online_merge(running, query_heads, key_block, value_block, key_start, length, score_scale):
    top_old, total_old, accum_old = running
    head_count = query_heads.shape[0]
    key_width = key_block.shape[0]
    key_heads = key_block.reshape(key_width, head_count, -1)
    value_heads = value_block.reshape(key_width, head_count, -1)
    scores = (
        jnp.einsum("hqd,khd->hqk", query_heads, key_heads, preferred_element_type=jnp.float32)
        * score_scale
    )
    usable = (key_start + jnp.arange(key_width, dtype=jnp.int32) < length)[None, None, :]
    masked = jnp.where(usable, scores, MASKED)
    top_new = jnp.maximum(top_old, jnp.max(masked, axis=-1))
    factor = jnp.exp(top_old - top_new)
    weights_here = jnp.where(usable, jnp.exp(masked - top_new[:, :, None]), 0.0)
    total_new = total_old * factor + jnp.sum(weights_here, axis=-1)
    accum_new = accum_old * factor[:, :, None] + jnp.einsum(
        "hqk,khd->hqd",
        weights_here.astype(jnp.bfloat16),
        value_heads,
        preferred_element_type=jnp.float32,
    )
    return (top_new, total_new, accum_new)


def score_grads(
    query_heads,
    grad_heads,
    log_total,
    row_delta,
    key_block,
    value_block,
    key_start,
    length,
    score_scale,
):
    head_count = query_heads.shape[0]
    key_width = key_block.shape[0]
    key_heads = key_block.reshape(key_width, head_count, -1)
    value_heads = value_block.reshape(key_width, head_count, -1)
    scores = (
        jnp.einsum("hqd,khd->hqk", query_heads, key_heads, preferred_element_type=jnp.float32)
        * score_scale
    )
    usable = (key_start + jnp.arange(key_width, dtype=jnp.int32) < length)[None, None, :]
    soft_weights = jnp.where(usable, jnp.exp(scores - log_total[:, :, None]), 0.0)
    grad_soft = jnp.einsum(
        "hqd,khd->hqk", grad_heads, value_heads, preferred_element_type=jnp.float32
    )
    grad_scores = (soft_weights * (grad_soft - row_delta[:, :, None])).astype(jnp.bfloat16)
    return (key_heads, grad_scores, soft_weights.astype(jnp.bfloat16))


def per_device(inputs, lengths, cotangent, w_qkv, w_out, w_in, w_back, vectors, ffn_bias):
    own_rows = inputs[0]
    row_count = own_rows.shape[0]
    model_width = own_rows.shape[1]
    head_count = HEADS
    head_size = model_width // head_count
    score_scale = head_size ** (-0.5)
    length = lengths[0]
    ctx_size = lax.axis_size("ctx")
    row_start = lax.axis_index("ctx") * row_count
    qkv_full, vector_full = (
        lax.all_gather(w_qkv, ("seq", "ctx"), axis=0, tiled=True),
        lax.all_gather(vectors, ("seq", "ctx"), axis=0, tiled=True),
    )
    vec = vector_full.astype(jnp.float32)
    projected = jnp.dot(own_rows, qkv_full, preferred_element_type=jnp.float32)
    query_rows = (projected[:, :model_width] + vec[:, 0]).astype(jnp.bfloat16)
    key_rows = projected[:, model_width : 2 * model_width].astype(jnp.bfloat16)
    value_rows = (projected[:, 2 * model_width :] + vec[:, 1]).astype(jnp.bfloat16)
    query_heads = to_heads(query_rows, head_count)
    start_state = (
        jnp.full((head_count, row_count), MASKED, jnp.float32),
        jnp.zeros((head_count, row_count), jnp.float32),
        jnp.zeros((head_count, row_count, head_size), jnp.float32),
    )
    running = start_state
    piece_start = jnp.int32(0)
    key_piece = lax.all_gather(key_rows, "ctx", axis=0, tiled=True)
    value_piece = lax.all_gather(value_rows, "ctx", axis=0, tiled=True)
    for offset, extent in key_spans(key_piece.shape[0]):
        running = online_merge(
            running,
            query_heads,
            key_piece[offset : offset + extent],
            value_piece[offset : offset + extent],
            piece_start + offset,
            length,
            score_scale,
        )
    row_top, row_total, accum = running
    out_full, in_full, back_full, ffn_full = (
        lax.all_gather(w_out, ("seq", "ctx"), axis=0, tiled=True),
        lax.all_gather(w_in, ("seq", "ctx"), axis=0, tiled=True),
        lax.all_gather(w_back, ("seq", "ctx"), axis=0, tiled=True),
        lax.all_gather(ffn_bias, ("seq", "ctx"), axis=0, tiled=True),
    )
    attended_f = accum / row_total[:, :, None]
    log_total = row_top + jnp.log(row_total)
    attended = attended_f.transpose(1, 0, 2).reshape(row_count, model_width).astype(jnp.bfloat16)
    branch = jnp.dot(attended, out_full, preferred_element_type=jnp.float32) + vec[:, 2]
    first_in = own_rows.astype(jnp.float32) + branch
    normed_first, first_back = jax.vjp(layer_norm, first_in, vec[:, 3], vec[:, 4])
    first_low = normed_first.astype(jnp.bfloat16)
    hidden = jnp.dot(first_low, in_full, preferred_element_type=jnp.float32) + ffn_full.astype(
        jnp.float32
    )
    active_f, gelu_back = jax.vjp(gelu_exact, hidden)
    active = active_f.astype(jnp.bfloat16)
    second = jnp.dot(active, back_full, preferred_element_type=jnp.float32) + vec[:, 5]
    result, second_back = jax.vjp(layer_norm, normed_first + second, vec[:, 6], vec[:, 7])
    valid_rows = (row_start + jnp.arange(row_count, dtype=jnp.int32) < length).astype(jnp.float32)[
        :, None
    ]
    grad_result = cotangent[0].astype(jnp.float32) * valid_rows
    grad_second, grad_gain_two, grad_shift_two = second_back(grad_result)
    grad_second_low = grad_second.astype(jnp.bfloat16)
    grad_active = jnp.dot(grad_second_low, back_full.T, preferred_element_type=jnp.float32)
    grad_w_back = jnp.dot(active.T, grad_second_low, preferred_element_type=jnp.float32)
    grad_hidden = gelu_back(grad_active)[0].astype(jnp.bfloat16)
    grad_w_in = jnp.dot(first_low.T, grad_hidden, preferred_element_type=jnp.float32)
    grad_first = grad_second + jnp.dot(grad_hidden, in_full.T, preferred_element_type=jnp.float32)
    grad_branch_full, grad_gain_one, grad_shift_one = first_back(grad_first)
    grad_branch = grad_branch_full.astype(jnp.bfloat16)
    grad_w_out = jnp.dot(attended.T, grad_branch, preferred_element_type=jnp.float32)
    grad_attended = jnp.dot(grad_branch, out_full.T, preferred_element_type=jnp.float32).astype(
        jnp.bfloat16
    )
    grad_heads = to_heads(grad_attended, head_count)
    row_delta = jnp.sum(grad_heads.astype(jnp.float32) * attended_f, axis=-1)
    zero_query = jnp.zeros((head_count, row_count, head_size), jnp.float32)
    key_all, value_all = (
        lax.all_gather(key_rows, "ctx", axis=0, tiled=True),
        lax.all_gather(value_rows, "ctx", axis=0, tiled=True),
    )
    group_size = 1
    while group_size * 2 * row_count <= 2048 and ctx_size % (group_size * 2) == 0:
        group_size = group_size * 2
    block_rows = group_size * row_count
    blocks_total = ctx_size // group_size

    def grad_step(grad_query, block_in):
        key_block, value_block, block_start = block_in
        key_heads, grad_scores, soft_low = score_grads(
            query_heads,
            grad_heads,
            log_total,
            row_delta,
            key_block,
            value_block,
            block_start,
            length,
            score_scale,
        )
        grad_query = (
            grad_query
            + jnp.einsum("hqk,khd->hqd", grad_scores, key_heads, preferred_element_type=jnp.float32)
            * score_scale
        )
        grad_key = (
            jnp.einsum("hqk,hqd->khd", grad_scores, query_heads, preferred_element_type=jnp.float32)
            * score_scale
        )
        grad_value = jnp.einsum(
            "hqk,hqd->khd", soft_low, grad_heads, preferred_element_type=jnp.float32
        )
        joined = jnp.concatenate(
            (
                grad_key.reshape(block_rows, model_width),
                grad_value.reshape(block_rows, model_width),
            ),
            axis=1,
        )
        return (grad_query, joined)

    block_starts = jnp.arange(blocks_total, dtype=jnp.int32) * block_rows
    grad_query, grad_terms = lax.scan(
        grad_step,
        zero_query,
        (
            key_all.reshape(blocks_total, block_rows, model_width),
            value_all.reshape(blocks_total, block_rows, model_width),
            block_starts,
        ),
    )
    owned = lax.psum_scatter(
        grad_terms.reshape(blocks_total * block_rows, 2 * model_width),
        "ctx",
        scatter_dimension=0,
        tiled=True,
    )
    grad_key_rows = owned[:, :model_width]
    grad_value_rows = owned[:, model_width:]
    grad_query_low = (
        grad_query.transpose(1, 0, 2).reshape(row_count, model_width).astype(jnp.bfloat16)
    )
    grad_key_low = grad_key_rows.astype(jnp.bfloat16)
    grad_value_low = grad_value_rows.astype(jnp.bfloat16)
    grad_projected = jnp.concatenate((grad_query_low, grad_key_low, grad_value_low), axis=1)
    grad_w_qkv = jnp.dot(own_rows.T, grad_projected, preferred_element_type=jnp.float32)
    grad_inputs = grad_branch_full + jnp.dot(
        grad_projected, qkv_full.T, preferred_element_type=jnp.float32
    )
    grad_vectors = jnp.stack(
        (
            jnp.sum(grad_query_low.astype(jnp.float32), axis=0),
            jnp.sum(grad_value_low.astype(jnp.float32), axis=0),
            jnp.sum(grad_branch.astype(jnp.float32), axis=0),
            grad_gain_one,
            grad_shift_one,
            jnp.sum(grad_second_low.astype(jnp.float32), axis=0),
            grad_gain_two,
            grad_shift_two,
        ),
        axis=1,
    )
    grad_ffn = jnp.sum(grad_hidden.astype(jnp.float32), axis=0)
    summed_grads = (
        lax.psum_scatter(grad_w_qkv, ("seq", "ctx"), scatter_dimension=0, tiled=True),
        lax.psum_scatter(grad_w_out, ("seq", "ctx"), scatter_dimension=0, tiled=True),
        lax.psum_scatter(grad_w_in, ("seq", "ctx"), scatter_dimension=0, tiled=True),
        lax.psum_scatter(grad_w_back, ("seq", "ctx"), scatter_dimension=0, tiled=True),
        lax.psum_scatter(grad_vectors, ("seq", "ctx"), scatter_dimension=0, tiled=True),
        lax.psum_scatter(grad_ffn, ("seq", "ctx"), scatter_dimension=0, tiled=True),
    )
    return (
        result.astype(jnp.bfloat16)[None],
        grad_inputs[None],
        summed_grads[0],
        summed_grads[1],
        summed_grads[2],
        summed_grads[3],
        summed_grads[4],
        summed_grads[5],
    )


def solution(mesh):
    return jax.shard_map(
        per_device,
        mesh=mesh,
        in_specs=(
            P("seq", "ctx", None),
            P("seq"),
            P("seq", "ctx", None),
            P(("seq", "ctx"), None),
            P(("seq", "ctx"), None),
            P(("seq", "ctx"), None),
            P(("seq", "ctx"), None),
            P(("seq", "ctx"), None),
            P(("seq", "ctx")),
        ),
        out_specs=(
            P("seq", "ctx", None),
            P("seq", "ctx", None),
            P(("seq", "ctx"), None),
            P(("seq", "ctx"), None),
            P(("seq", "ctx"), None),
            P(("seq", "ctx"), None),
            P(("seq", "ctx"), None),
            P(("seq", "ctx")),
        ),
        check_vma=False,
    )
```

profile of v0, /device:TPU:0, one launch (start us, length us, event | category | flops | bytes accessed | tf_op | source)
XLA Modules:
  0.0 1052.9 jit_solution(521782439624674951)
XLA Ops:
  7.9 43.8 %all-gather = bf16[32,24,8]{1,2,0:T(8,128)(2,1)S(1)} all-gather(bf16[1,24,8]{1,2,0:T(8,128)(2,1)} %bitcast.104), channel_id=1, replica_groups=mesh['seq'=2,'ctx'=16] {'seq','ctx'}, dimensions={0}, use_global_device_ids=true | all-gather | bytes 12672 | tf_op jit(solution)/shard_map/all_gather | solution.py:100
  52.1 21.5 %all-gather.8.cloned.1.call-done = bf16[768,2304]{1,0:T(8,128)(2,1)} async-done(((bf16[24,2304]{1,0:T(8,128)(2,1)}), bf16[768,2304]{1,0:T(8,128)(2,1)}) %all-gather.8.cloned.1.call-update) | async-done | bytes 3538960 | tf_op jit(solution)/shard_map/all_gather | solution.py:99
  73.6 2.8 fusion.36
  80.7 39.0 %all-reduce = bf16[3072]{0:T(1024)(128)(2,1)S(1)} all-reduce(bf16[3072]{0:T(1024)(128)(2,1)S(1)} %dynamic-update-slice), channel_id=1, replica_groups=mesh['seq'=2,'ctx'=16] {'seq','ctx'}, use_global_device_ids=true, to_apply=%add | all-reduce | flops 3072 | bytes 12288
  120.4 1.2 all-gather.12.cloned.1.call-done
  121.6 4.7 copy.40
  126.3 42.0 %all-gather.10.cloned.1.call-done = bf16[2048,768]{1,0:T(8,128)(2,1)} async-done(((bf16[128,768]{1,0:T(8,128)(2,1)}), bf16[2048,768]{1,0:T(8,128)(2,1)}) %all-gather.10.cloned.1.call-update) | async-done | bytes 3145744 | tf_op jit(solution)/shard_map/all_gather | solution.py:115
  168.2 4.7 copy.39
  173.0 3.9 select_reduce_fusion
  176.9 3.2 fusion.1
  180.2 1.3 copy-done
  181.4 5.6 fusion.32
  187.0 36.4 %all-gather.14.cloned.1.call-done = bf16[768,768]{1,0:T(8,128)(2,1)} async-done(((bf16[24,768]{1,0:T(8,128)(2,1)}), bf16[768,768]{1,0:T(8,128)(2,1)}) %all-gather.14.cloned.1.call-update) | async-done | bytes 1179664 | tf_op jit(solution)/shard_map/all_gather | solution.py:129
  223.4 1.8 fusion.55
  225.5 63.2 %all-gather.16.cloned.1.call-done = bf16[768,3072]{1,0:T(8,128)(2,1)} async-done(((bf16[24,3072]{1,0:T(8,128)(2,1)}), bf16[768,3072]{1,0:T(8,128)(2,1)}) %all-gather.16.cloned.1.call-update) | async-done | bytes 4718608 | tf_op jit(solution)/shard_map/all_gather | solution.py:130
  288.7 8.4 multiply_convert_fusion.1
  297.1 56.3 %all-gather.18.cloned.1.call-done = bf16[3072,768]{1,0:T(8,128)(2,1)} async-done(((bf16[96,768]{1,0:T(8,128)(2,1)}), bf16[3072,768]{1,0:T(8,128)(2,1)}) %all-gather.18.cloned.1.call-update) | async-done | bytes 4718608 | tf_op jit(solution)/shard_map/all_gather | solution.py:131
  353.4 3.4 fusion.56
  357.3 0.9 fusion.53
  358.9 2.5 convert_reduce_fusion
  361.4 2.4 multiply_reduce_fusion
  366.2 9.9 fusion.3
  376.3 7.3 multiply_convert_fusion
  383.6 4.1 convolution_multiply_fusion
  388.2 11.4 %pad_maximum_fusion = f32[2048,1536]{0,1:T(8,128)} fusion(f32[2048,768]{0,1:T(8,128)} %bitcast.88, f32[2048,768]{0,1:T(8,128)} %bitcast.85), kind=kLoop, calls=%fused_computation | loop fusion | flops 3145728 | bytes 25165824 | tf_op jit(solution)/shard_map/while/body/eval_jaxpr/concatenate | solution.py:203
  399.6 0.9 copy-done.10
  400.5 1.9 fusion.57
  402.7 6.1 fusion.49
  408.9 6.0 fusion.58
  415.0 2.3 copy-done.2
  417.3 6.6 convert_reduce_fusion.4
  423.8 108.9 %reduce-scatter.9.cloned.1.call-done = f32[128,1536]{0,1:T(8,128)} async-done(((f32[2048,1536]{0,1:T(8,128)}), f32[128,1536]{0,1:T(8,128)}) %reduce-scatter.9.cloned.1.call-update) | async-done | bytes 786448 | tf_op jit(solution)/shard_map/reduce_scatter | solution.py:222
  532.8 1.2 convert.9
  534.7 5.0 convolution_bitcast_fusion
  539.6 8.0 copy.43
  548.3 1.0 stack.32
  549.3 1.3 stack.30
  550.6 1.3 stack.31
  551.9 1.3 stack.29
  553.8 1.1 convert_reduce_fusion.3
  554.9 1.4 stack.35
  556.2 40.7 %all-reduce.3 = (f32[768,8]{0,1:T(8,128)}, f32[3072]{0:T(1024)S(1)}) all-reduce(f32[768,8]{0,1:T(8,128)} %stack.35, f32[3072]{0:T(1024)} %get-tuple-element.86), channel_id=7, replica_groups=mesh['seq'=2,'ctx'=16] {'seq','ctx'}, use_global_device_ids=true, to_apply=%region_24.25.clone | all-reduce | flops 9216 | bytes 73728
  597.5 1.4 constant_dynamic-slice_fusion
  598.9 3.3 fusion.19
  602.1 35.7 %reduce-scatter.11.cloned.1.call-done = f32[24,768]{1,0:T(8,128)} async-done(((f32[768,768]{1,0:T(8,128)}), f32[24,768]{1,0:T(8,128)}) %reduce-scatter.11.cloned.1.call-update) | async-done | bytes 73744 | tf_op jit(solution)/shard_map/reduce_scatter | solution.py:256
  637.8 142.0 %reduce-scatter.13.cloned.1.call-done = f32[24,3072]{1,0:T(8,128)} async-done(((f32[768,3072]{1,0:T(8,128)}), f32[24,3072]{1,0:T(8,128)}) %reduce-scatter.13.cloned.1.call-update) | async-done | bytes 294928 | tf_op jit(solution)/shard_map/reduce_scatter | solution.py:257
  779.8 141.8 %reduce-scatter.15.cloned.1.call-done = f32[96,768]{1,0:T(8,128)} async-done(((f32[3072,768]{1,0:T(8,128)}), f32[96,768]{1,0:T(8,128)}) %reduce-scatter.15.cloned.1.call-update) | async-done | bytes 294928 | tf_op jit(solution)/shard_map/reduce_scatter | solution.py:258
  921.6 124.7 %reduce-scatter.17.cloned.1.call-done = f32[24,2304]{1,0:T(8,128)} async-done(((f32[768,2304]{1,0:T(8,128)}), f32[24,2304]{1,0:T(8,128)}) %reduce-scatter.17.cloned.1.call-update) | async-done | bytes 221200
  (100 shorter events, 12.8 us)
Async XLA Ops:
  7.2 66.5 %all-gather.8.cloned.1.call-start = ((), (), s32[]{:S(2)}) async-start(), calls=%async_computation.5 | async-start | bytes 3649536 | tf_op jit(solution)/shard_map/all_gather | solution.py:99
  7.9 113.7 %all-gather.12.cloned.1.call-start = ((), (), s32[]{:S(2)}) async-start(), calls=%async_computation.7 | async-start | bytes 3342336 | tf_op jit(solution)/shard_map/all_gather | solution.py:116
  76.4 4.0 copy-start.14
  77.2 91.1 %all-gather.10.cloned.1.call-start = ((), (), s32[]{:S(2)}) async-start(), calls=%async_computation.6 | async-start | bytes 3342336 | tf_op jit(solution)/shard_map/all_gather | solution.py:115
  77.9 145.5 %all-gather.14.cloned.1.call-start = ((), (), s32[]{:S(2)}) async-start(), calls=%async_computation.8 | async-start | bytes 1216512 | tf_op jit(solution)/shard_map/all_gather | solution.py:129
  78.5 210.2 %all-gather.16.cloned.1.call-start = ((), (), s32[]{:S(2)}) async-start(), calls=%async_computation.9 | async-start | bytes 4866048 | tf_op jit(solution)/shard_map/all_gather | solution.py:130
  79.1 274.3 %all-gather.18.cloned.1.call-start = ((), (), s32[]{:S(2)}) async-start(), calls=%async_computation.10 | async-start | bytes 4866048 | tf_op jit(solution)/shard_map/all_gather | solution.py:131
  79.7 453.1 %reduce-scatter.9.cloned.1.call-start = ((), (), s32[]{:S(2)}) async-start(), calls=%async_computation.11 | async-start | bytes 13369344 | tf_op jit(solution)/shard_map/reduce_scatter | solution.py:222
  176.9 4.6 copy-start
  181.4 42.0 %copy-start.8 = (bf16[1,128,768]{2,1,0:T(8,128)(2,1)S(1)}, bf16[1,128,768]{2,1,0:T(8,128)(2,1)}, u32[]{:S(2)}) copy-start(bf16[1,128,768]{2,1,0:T(8,128)(2,1)} %param.9) | copy-start | bytes 589828
  353.4 5.5 slice-start
  353.4 3.6 copy-start.9
  353.4 3.6 copy-start.12
  353.4 5.5 slice-start.1
  353.4 5.5 copy-start.16
  356.8 2.2 copy-start.15
  358.2 3.2 slice-start.2
  358.9 2.5 slice-start.3
  363.8 1.7 copy-start.5
  364.0 0.8 copy-start.6
  364.1 12.1 %copy-start.13 = (f32[128]{0:T(128)}, f32[128]{0:T(128)S(1)}, u32[]{:S(2)}) copy-start(f32[128]{0:T(128)S(1)} %negate_multiply_fusion.1) | copy-start | bytes 1540
  366.2 9.9 copy-start.11
  366.2 10.0 copy-start.7
  383.6 4.6 copy-start.1
  399.5 0.9 copy-start.10
  399.6 238.3 %reduce-scatter.11.cloned.1.call-start = ((), (), s32[]{:S(2)}) async-start(), calls=%async_computation.12 | async-start | bytes 2433024 | tf_op jit(solution)/shard_map/reduce_scatter | solution.py:256
  402.4 377.4 %reduce-scatter.13.cloned.1.call-start = ((), (), s32[]{:S(2)}) async-start(), calls=%async_computation.13 | async-start | bytes 9732096 | tf_op jit(solution)/shard_map/reduce_scatter | solution.py:257
  408.8 512.8 %reduce-scatter.15.cloned.1.call-start = ((), (), s32[]{:S(2)}) async-start(), calls=%async_computation.14 | async-start | bytes 9732096 | tf_op jit(solution)/shard_map/reduce_scatter | solution.py:258
  414.9 2.4 copy-start.2
  414.9 631.4 %reduce-scatter.17.cloned.1.call-start = ((), (), s32[]{:S(2)}) async-start(), calls=%async_computation.15 | async-start | bytes 7299072
  533.9 0.7 copy-start.4
  547.7 51.2 %copy-start.3 = (bf16[768,2304]{1,0:T(8,128)(2,1)S(1)}, bf16[768,2304]{1,0:T(8,128)(2,1)}, u32[]{:S(2)}) copy-start(bf16[768,2304]{1,0:T(8,128)(2,1)} %all-gather.8.cloned.1.call-done) | copy-start | bytes 10616836
Sparse Core Ops, SparseCore 0:
  10.9 62.7 all-gather.7
  77.3 44.2 all-gather.11
  124.4 43.7 all-gather.9
  171.0 52.3 all-gather.13
  226.2 62.4 all-gather.15
  291.4 61.8 all-gather.17
  399.7 133.0 reduce-scatter.8
  538.6 99.1 reduce-scatter.10
  644.3 135.4 reduce-scatter.12
  786.1 135.4 reduce-scatter.14
  927.9 118.3 reduce-scatter.16
where the time goes:
time: 1050 us
  waiting for transfers between devices  776 us (74%)
  blocking collectives  123 us (12%)
  matrix products  81.4 us (8%)
  local copies, waits for them, and re-layouts  35 us (3%)
  other arithmetic  21.5 us (2%)
  between operations  14.8 us (1%)
    reduce_scatter x1, waiting for transfers between devices, per_device(): lax.psum_scatter(grad_w_in, ('seq', 'ctx'), scatter_dimension=0, tiled=True)  142 us
    reduce_scatter x1, waiting for transfers between devices, per_device(): lax.psum_scatter(grad_w_back, ('seq', 'ctx'), scatter_dimension=0, tiled=...  142 us
    unnamed x12, waiting for transfers between devices  127 us
    reduce_scatter x1, waiting for transfers between devices, per_device(): lax.psum_scatter(grad_terms.reshape(blocks_total * block_rows, 2 * model_...  109 us
    unnamed x2, blocking collectives  79.7 us
    all_gather x1, waiting for transfers between devices, per_device(): lax.all_gather(w_in, ('seq', 'ctx'), axis=0, tiled=True)  63.2 us
    all_gather x1, waiting for transfers between devices, per_device(): lax.all_gather(w_back, ('seq', 'ctx'), axis=0, tiled=True)  56.3 us
    all_gather x1, blocking collectives, per_device(): lax.all_gather(vectors, ('seq', 'ctx'), axis=0, tiled=True)  43.8 us
  transfers between devices with their start and end apart: 11, of which 11 were waited for; matrix products, arithmetic and copies ran while one was open for 8% of the time, Pallas kernels for 0%

commit v1 on v0

--- a/solution.py
+++ b/solution.py
@@ -112,8 +112,11 @@
     )
     running = start_state
     piece_start = jnp.int32(0)
-    key_piece = lax.all_gather(key_rows, "ctx", axis=0, tiled=True)
-    value_piece = lax.all_gather(value_rows, "ctx", axis=0, tiled=True)
+    key_piece, value_piece = jnp.split(
+        lax.all_gather(jnp.concatenate([key_rows, value_rows], axis=1), "ctx", axis=0, tiled=True),
+        [key_rows.shape[1]],
+        axis=1,
+    )
     for offset, extent in key_spans(key_piece.shape[0]):
         running = online_merge(
             running,

time: 1050 us -> 1120 us (1.067)
  waiting for transfers between devices: 776 us -> 820 us
  local copies, waits for them, and re-layouts: 35 us -> 46.7 us
    all_gather x2 -> x3, waiting for transfers between devices: 43.2 us -> 93.4 us  [the longest x1 52.9 us: per_device(): lax.all_gather(jnp.concatenate([key_rows, value_rows], axis=1), 'ctx', ax...]
    split x0 -> x3, local copies, waits for them, and re-layouts: none -> 12.5 us  [per_device(): jnp.split(lax.all_gather(jnp.concatenate([key_rows, value_rows], axis=1),...]
    unnamed x12 -> x13, waiting for transfers between devices: 127 us -> 127 us
  transfers between devices with their start and end apart: 11 -> 12, of which waited for: 11 -> 11; matrix products, arithmetic and copies ran while one was open for 8% -> 9% of each run, Pallas kernels for 0% -> 0%
where the time goes in v1:
time: 1120 us
  waiting for transfers between devices  820 us (73%)
  blocking collectives  123 us (11%)
  matrix products  87 us (8%)
  local copies, waits for them, and re-layouts  46.7 us (4%)
  other arithmetic  25.7 us (2%)
  between operations  15.4 us (1%)
    reduce_scatter x1, waiting for transfers between devices, per_device(): lax.psum_scatter(grad_w_back, ('seq', 'ctx'), scatter_dimension=0, tiled=...  142 us
    reduce_scatter x1, waiting for transfers between devices, per_device(): lax.psum_scatter(grad_w_in, ('seq', 'ctx'), scatter_dimension=0, tiled=True)  142 us
    unnamed x13, waiting for transfers between devices  127 us
    reduce_scatter x1, waiting for transfers between devices, per_device(): lax.psum_scatter(grad_terms.reshape(blocks_total * block_rows, 2 * model_...  109 us
    unnamed x2, blocking collectives  79.7 us
    all_gather x1, waiting for transfers between devices, per_device(): lax.all_gather(w_in, ('seq', 'ctx'), axis=0, tiled=True)  63.2 us
    all_gather x1, waiting for transfers between devices, per_device(): lax.all_gather(w_back, ('seq', 'ctx'), axis=0, tiled=True)  56.4 us
    all_gather x1, waiting for transfers between devices, per_device(): lax.all_gather(jnp.concatenate([key_rows, value_rows], axis=1), 'ctx', ax...  52.9 us
  transfers between devices with their start and end apart: 12, of which 11 were waited for; matrix products, arithmetic and copies ran while one was open for 9% of the time, Pallas kernels for 0%

profile of v1, /device:TPU:0, one launch (start us, length us, event | category | flops | bytes accessed | tf_op | source)
XLA Modules:
  0.0 1118.6 jit_solution(12157068863562952093)
XLA Ops:
  7.9 43.8 %all-gather = bf16[32,24,8]{1,2,0:T(8,128)(2,1)S(1)} all-gather(bf16[1,24,8]{1,2,0:T(8,128)(2,1)} %bitcast.110), channel_id=1, replica_groups=mesh['seq'=2,'ctx'=16] {'seq','ctx'}, dimensions={0}, use_global_device_ids=true | all-gather | bytes 12672 | tf_op jit(solution)/shard_map/all_gather | solution.py:100
  52.7 20.9 %all-gather.9.cloned.1.call-done = bf16[768,2304]{1,0:T(8,128)(2,1)} async-done(((bf16[24,2304]{1,0:T(8,128)(2,1)}), bf16[768,2304]{1,0:T(8,128)(2,1)}) %all-gather.9.cloned.1.call-update) | async-done | bytes 3538960 | tf_op jit(solution)/shard_map/all_gather | solution.py:99
  73.6 2.8 fusion.37
  78.0 1.8 pad_maximum_fusion.2
  82.7 39.1 %all-reduce = bf16[3072]{0:T(1024)(128)(2,1)S(1)} all-reduce(bf16[3072]{0:T(1024)(128)(2,1)S(1)} %dynamic-update-slice), channel_id=1, replica_groups=mesh['seq'=2,'ctx'=16] {'seq','ctx'}, use_global_device_ids=true, to_apply=%add | all-reduce | flops 3072 | bytes 12288
  123.1 4.7 copy.48
  127.8 40.5 %all-gather.19.cloned.1.call-done = bf16[2048,768]{1,0:T(8,128)(2,1)} async-done(((bf16[128,768]{1,0:T(8,128)(2,1)}), bf16[2048,768]{1,0:T(8,128)(2,1)}) %all-gather.19.cloned.1.call-update) | async-done | bytes 3145744 | tf_op jit(solution)/shard_map/all_gather | solution.py:172
  168.3 3.2 copy.46
  171.5 6.4 fusion.59
  177.9 52.9 %all-gather.11.cloned.1.call-done = bf16[2048,1536]{1,0:T(8,128)(2,1)} async-done(((bf16[128,1536]{1,0:T(8,128)(2,1)}), bf16[2048,1536]{1,0:T(8,128)(2,1)}) %all-gather.11.cloned.1.call-update) | async-done | bytes 6291472 | tf_op jit(solution)/shard_map/all_gather | solution.py:116
  230.8 4.9 fusion.56
  235.7 4.7 copy.44
  240.4 2.9 copy.45
  243.3 3.8 fusion
  247.2 3.2 fusion.2
  251.1 5.6 fusion.33
  256.7 29.5 %all-gather.13.cloned.1.call-done = bf16[768,768]{1,0:T(8,128)(2,1)} async-done(((bf16[24,768]{1,0:T(8,128)(2,1)}), bf16[768,768]{1,0:T(8,128)(2,1)}) %all-gather.13.cloned.1.call-update) | async-done | bytes 1179664 | tf_op jit(solution)/shard_map/all_gather | solution.py:132
  286.2 1.8 fusion.57
  288.3 63.2 %all-gather.15.cloned.1.call-done = bf16[768,3072]{1,0:T(8,128)(2,1)} async-done(((bf16[24,3072]{1,0:T(8,128)(2,1)}), bf16[768,3072]{1,0:T(8,128)(2,1)}) %all-gather.15.cloned.1.call-update) | async-done | bytes 4718608 | tf_op jit(solution)/shard_map/all_gather | solution.py:133
  351.5 8.4 multiply_convert_fusion.1
  359.9 56.4 %all-gather.17.cloned.1.call-done = bf16[3072,768]{1,0:T(8,128)(2,1)} async-done(((bf16[96,768]{1,0:T(8,128)(2,1)}), bf16[3072,768]{1,0:T(8,128)(2,1)}) %all-gather.17.cloned.1.call-update) | async-done | bytes 4718608 | tf_op jit(solution)/shard_map/all_gather | solution.py:134
  416.4 3.4 fusion.58
  422.5 2.4 convert_reduce_fusion
  425.0 2.4 multiply_reduce_fusion
  429.0 1.2 convolution_convert_fusion
  431.4 9.9 fusion.4
  441.5 7.5 multiply_convert_fusion
  449.0 4.1 convolution_multiply_fusion
  453.6 11.4 %pad_maximum_fusion = f32[2048,1536]{0,1:T(8,128)} fusion(f32[2048,768]{0,1:T(8,128)} %bitcast.92, f32[2048,768]{0,1:T(8,128)} %bitcast.91), kind=kLoop, calls=%fused_computation | loop fusion | flops 3145728 | bytes 25165824 | tf_op jit(solution)/shard_map/while/body/eval_jaxpr/concatenate | solution.py:206
  465.9 1.9 fusion.60
  467.9 6.0 fusion.50
  474.9 6.0 fusion.61
  481.0 2.3 copy-done.1
  483.3 6.0 convert_reduce_fusion.4
  489.3 109.0 %reduce-scatter.9.cloned.1.call-done = f32[128,1536]{0,1:T(8,128)} async-done(((f32[2048,1536]{0,1:T(8,128)}), f32[128,1536]{0,1:T(8,128)}) %reduce-scatter.9.cloned.1.call-update) | async-done | bytes 786448 | tf_op jit(solution)/shard_map/reduce_scatter | solution.py:225
  600.2 4.0 convolution_bitcast_fusion
  604.2 8.0 copy.50
  614.2 1.3 stack.30
  615.4 1.3 stack.31
  616.7 1.3 stack.29
  619.7 1.3 stack.35
  621.1 40.6 %all-reduce.3 = (f32[768,8]{0,1:T(8,128)}, f32[3072]{0:T(1024)S(1)}) all-reduce(f32[768,8]{0,1:T(8,128)} %stack.35, f32[3072]{0:T(1024)} %get-tuple-element.86), channel_id=7, replica_groups=mesh['seq'=2,'ctx'=16] {'seq','ctx'}, use_global_device_ids=true, to_apply=%region_24.25.clone | all-reduce | flops 9216 | bytes 73728
  662.3 1.4 constant_dynamic-slice_fusion
  663.6 3.3 fusion.20
  666.9 36.5 %reduce-scatter.11.cloned.1.call-done = f32[24,768]{1,0:T(8,128)} async-done(((f32[768,768]{1,0:T(8,128)}), f32[24,768]{1,0:T(8,128)}) %reduce-scatter.11.cloned.1.call-update) | async-done | bytes 73744 | tf_op jit(solution)/shard_map/reduce_scatter | solution.py:259
  703.4 141.8 %reduce-scatter.13.cloned.1.call-done = f32[24,3072]{1,0:T(8,128)} async-done(((f32[768,3072]{1,0:T(8,128)}), f32[24,3072]{1,0:T(8,128)}) %reduce-scatter.13.cloned.1.call-update) | async-done | bytes 294928 | tf_op jit(solution)/shard_map/reduce_scatter | solution.py:260
  845.2 141.9 %reduce-scatter.15.cloned.1.call-done = f32[96,768]{1,0:T(8,128)} async-done(((f32[3072,768]{1,0:T(8,128)}), f32[96,768]{1,0:T(8,128)}) %reduce-scatter.15.cloned.1.call-update) | async-done | bytes 294928 | tf_op jit(solution)/shard_map/reduce_scatter | solution.py:261
  987.1 124.7 %reduce-scatter.17.cloned.1.call-done = f32[24,2304]{1,0:T(8,128)} async-done(((f32[768,2304]{1,0:T(8,128)}), f32[24,2304]{1,0:T(8,128)}) %reduce-scatter.17.cloned.1.call-update) | async-done | bytes 221200
  (154 shorter events, 21.8 us)
Async XLA Ops:
  7.2 66.5 %all-gather.9.cloned.1.call-start = ((), (), s32[]{:S(2)}) async-start(), calls=%async_computation.5 | async-start | bytes 3649536 | tf_op jit(solution)/shard_map/all_gather | solution.py:99
  7.9 115.2 %all-gather.21.cloned.1.call-start = ((), (), s32[]{:S(2)}) async-start(), calls=%async_computation.11 | async-start | bytes 3342336 | tf_op jit(solution)/shard_map/all_gather | solution.py:173
  76.4 6.0 copy-start.37
  77.2 91.1 %all-gather.19.cloned.1.call-start = ((), (), s32[]{:S(2)}) async-start(), calls=%async_computation.10 | async-start | bytes 3342336 | tf_op jit(solution)/shard_map/all_gather | solution.py:172
  77.9 152.8 %all-gather.11.cloned.1.call-start = ((), (), s32[]{:S(2)}) async-start(), calls=%async_computation.6 | async-start | bytes 6684672 | tf_op jit(solution)/shard_map/all_gather | solution.py:116
  79.8 206.4 %all-gather.13.cloned.1.call-start = ((), (), s32[]{:S(2)}) async-start(), calls=%async_computation.7 | async-start | bytes 1216512 | tf_op jit(solution)/shard_map/all_gather | solution.py:132
  80.4 271.1 %all-gather.15.cloned.1.call-start = ((), (), s32[]{:S(2)}) async-start(), calls=%async_computation.8 | async-start | bytes 4866048 | tf_op jit(solution)/shard_map/all_gather | solution.py:133
  81.0 335.4 %all-gather.17.cloned.1.call-start = ((), (), s32[]{:S(2)}) async-start(), calls=%async_computation.9 | async-start | bytes 4866048 | tf_op jit(solution)/shard_map/all_gather | solution.py:134
  81.7 516.5 %reduce-scatter.9.cloned.1.call-start = ((), (), s32[]{:S(2)}) async-start(), calls=%async_computation.12 | async-start | bytes 13369344 | tf_op jit(solution)/shard_map/reduce_scatter | solution.py:225
  122.9 128.2 %copy-start.20 = (pred[2048]{0:T(1024)(128)(4,1)}, pred[2048]{0:T(1024)(128)(4,1)S(1)}, u32[]{:S(2)}) copy-start(pred[2048]{0:T(1024)(128)(4,1)S(1)} %iota_compare_fusion) | copy-start | bytes 6148
  171.5 6.4 copy-start
  251.1 35.2 %copy-start.10 = (bf16[1,128,768]{2,1,0:T(8,128)(2,1)S(1)}, bf16[1,128,768]{2,1,0:T(8,128)(2,1)}, u32[]{:S(2)}) copy-start(bf16[1,128,768]{2,1,0:T(8,128)(2,1)} %param.9) | copy-start | bytes 589828
  251.1 35.2 %copy-start.26 = (f32[768]{0:T(1024)S(1)}, f32[768]{0:T(1024)}, u32[]{:S(2)}) copy-start(f32[768]{0:T(1024)} %get-tuple-element.81) | copy-start | bytes 9220
  256.7 94.8 %copy-start.32 = (f32[3072]{0:T(1024)S(1)}, f32[3072]{0:T(1024)}, u32[]{:S(2)}) copy-start(f32[3072]{0:T(1024)} %convert_element_type.108) | copy-start | bytes 36868
  288.1 136.9 %copy-start.22 = (f32[128]{0:T(128)}, f32[128]{0:T(128)S(1)}, u32[]{:S(2)}) copy-start(f32[128]{0:T(128)S(1)} %broadcast_multiply_fusion.1) | copy-start | bytes 1540
  288.3 71.6 %copy-start.35 = (f32[128]{0:T(128)}, f32[128]{0:T(128)S(1)}, u32[]{:S(2)}) copy-start(f32[128]{0:T(128)S(1)} %multiply_reduce_fusion.4) | copy-start | bytes 1540
  288.3 128.0 %copy-start.29 = (f32[128]{0:T(128)}, f32[128]{0:T(128)S(1)}, u32[]{:S(2)}) copy-start(f32[128]{0:T(128)S(1)} %fusion.39) | copy-start | bytes 1540
  351.5 64.8 %copy-start.25 = (f32[768]{0:T(1024)S(1)}, f32[768]{0:T(1024)}, u32[]{:S(2)}) copy-start(f32[768]{0:T(1024)} %get-tuple-element.78) | copy-start | bytes 9220
  416.3 6.1 slice-start
  416.3 3.6 copy-start.12
  416.4 3.6 copy-start.33
  416.4 4.5 copy-start.24
  416.4 6.1 slice-start.1
  416.4 6.1 copy-start.39
  419.8 2.7 copy-start.38
  421.8 3.2 slice-start.2
  422.5 2.5 copy-start.14
  422.5 2.5 slice-start.3
  422.5 2.5 copy-start.30
  425.0 2.4 copy-start.8
  425.0 4.0 copy-start.5
  427.4 4.0 copy-start.17
  428.3 13.0 %copy-start.6 = (f32[128,768]{1,0:T(8,128)}, f32[128,768]{1,0:T(8,128)S(1)}, u32[]{:S(2)}) copy-start(f32[128,768]{1,0:T(8,128)S(1)} %get-tuple-element.93) | copy-start | bytes 1179652
  431.4 10.0 copy-start.16
  431.4 10.0 copy-start.18
  431.4 10.0 copy-start.19
  431.4 10.1 copy-start.7
  431.4 10.1 copy-start.21
  449.0 4.6 copy-start.2
  465.0 2.9 copy-start.9
  465.0 2.9 copy-start.23
  465.0 2.9 copy-start.31
  465.0 238.3 %reduce-scatter.11.cloned.1.call-start = ((), (), s32[]{:S(2)}) async-start(), calls=%async_computation.13 | async-start | bytes 2433024 | tf_op jit(solution)/shard_map/reduce_scatter | solution.py:259
  467.8 377.4 %reduce-scatter.13.cloned.1.call-start = ((), (), s32[]{:S(2)}) async-start(), calls=%async_computation.14 | async-start | bytes 9732096 | tf_op jit(solution)/shard_map/reduce_scatter | solution.py:260
  474.0 513.1 %reduce-scatter.15.cloned.1.call-start = ((), (), s32[]{:S(2)}) async-start(), calls=%async_computation.15 | async-start | bytes 9732096 | tf_op jit(solution)/shard_map/reduce_scatter | solution.py:261
  480.9 630.8 %reduce-scatter.17.cloned.1.call-start = ((), (), s32[]{:S(2)}) async-start(), calls=%async_computation.16 | async-start | bytes 7299072
  489.3 114.9 %copy-start.11 = (bf16[12,128,64]{1,2,0:T(8,128)(2,1)}, bf16[12,128,64]{1,2,0:T(8,128)(2,1)S(1)}, u32[]{:S(2)}) copy-start(bf16[12,128,64]{1,2,0:T(8,128)(2,1)S(1)} %get-tuple-element.120) | copy-start | bytes 589828
  612.2 51.4 %copy-start.3 = (bf16[768,2304]{1,0:T(8,128)(2,1)S(1)}, bf16[768,2304]{1,0:T(8,128)(2,1)}, u32[]{:S(2)}) copy-start(bf16[768,2304]{1,0:T(8,128)(2,1)} %all-gather.9.cloned.1.call-done) | copy-start | bytes 10616836
  (8 other events, 10.1 us)
Sparse Core Ops, SparseCore 0:
  10.9 62.7 all-gather.8
  77.3 44.2 all-gather.20
  124.5 43.7 all-gather.18
  171.0 59.7 all-gather.10
  233.5 52.6 all-gather.12
  289.0 62.4 all-gather.14
  354.4 61.8 all-gather.16
  465.1 133.0 reduce-scatter.8
  604.1 99.2 reduce-scatter.10
  709.7 135.4 reduce-scatter.12
  851.7 135.3 reduce-scatter.14
  993.2 118.5 reduce-scatter.16
